TPU v7x, 32 devices: a whole 2x2x4 slice. The times are simulated.
32 devices in a mesh: expert: 4 (over z), tensor: 8 (over y, x, core).
Axes of the slice: x: 2, y: 2, z: 4, core: 2. Of those that a mesh axis runs over, the one named last changes fastest.
Arguments:
- tokens: bfloat16 [512, 6144], P('expert', 'tensor'), may hold values from -6 to 6
- out_grad: bfloat16 [512, 6144], P('expert', 'tensor'), may hold values from -6 to 6
- expert_ids: int32 [512, 2], P('expert'), may hold values from 0 to 3, all different within a row; in each aligned block of 128 rows (0 to 127, 128 to 255, ...) at most 80 rows name the same one
- route_logits: float32 [512, 2], P('expert'), may hold values from -6 to 6
- w_gate: bfloat16 [4, 6144, 8192], P('expert', 'tensor'), may hold values from -0.078125 to 0.078125
- w_up: bfloat16 [4, 6144, 8192], P('expert', 'tensor'), may hold values from -0.078125 to 0.078125
- w_down: bfloat16 [4, 6144, 8192], P('expert', 'tensor'), may hold values from -0.0625 to 0.0625
- gate_scale: float32 [4, 8192], P('expert', 'tensor'), may hold values from 0.5 to 2
- up_scale: float32 [4, 8192], P('expert', 'tensor'), may hold values from 0.5 to 2
- down_scale: float32 [4, 8192], P('expert', 'tensor'), may hold values from 0.5 to 2
Outputs:
- mixed: bfloat16 [512, 6144], P('expert', 'tensor')
- token_grad: bfloat16 [512, 6144], P('expert', 'tensor')
- logit_grad: float32 [512, 2], P('expert')
- gate_grad: bfloat16 [4, 6144, 8192], P('expert', None, 'tensor')
- up_grad: bfloat16 [4, 6144, 8192], P('expert', None, 'tensor')
- down_grad: bfloat16 [4, 6144, 8192], P('expert', None, 'tensor')
Inputs may be any that keep to these rules, and one draw needn't show every extreme that they name: `expert_ids`: each token names two different experts; among the 128 tokens of one index of the expert axis, each expert is named by at most 80.
All inputs are finite; a program needn't handle non-finite values.
Results may differ from a plain program's by a relative error of at most 0.025.
Values may be sent and summed in bfloat16 or wider, within the bound.
A program may use at most 256 MiB of HBM per device.

v0:
```python
import jax
import jax.numpy as jnp
from jax import lax
from jax.sharding import PartitionSpec as P


def gate_tables(expert_ids, route_logits, count):
    first = jax.nn.sigmoid(route_logits[:, 0] - route_logits[:, 1])
    probs = jnp.stack([first, 1.0 - first], axis=1)
    labels = jnp.arange(count, dtype=jnp.int32)
    chosen = (expert_ids[:, :, None] == labels[None, None, :]).astype(jnp.float32)
    per_expert = jnp.sum(probs[:, :, None] * chosen, axis=1)
    member = jnp.sum(chosen, axis=1)
    return (probs, chosen, per_expert, member)


def contract_rows(left, right):
    return lax.dot_general(
        left, right, (((0,), (0,)), ((), ())), preferred_element_type=jnp.float32
    )


def body(
    tokens,
    out_grad,
    expert_ids,
    route_logits,
    w_gate,
    w_up,
    w_down,
    gate_scale,
    up_scale,
    down_scale,
):
    groups = lax.axis_size("expert")
    local_tokens, feat_width = tokens.shape
    probs, chosen, per_expert, member = gate_tables(expert_ids, route_logits, groups)
    member_cols = member.T.astype(jnp.bfloat16)[:, :, None]
    weight_cols = per_expert.T[:, :, None]

    def unpacking(packed):
        return packed.astype(jnp.float32)

    total_rows = groups * local_tokens
    send_rows = tokens[None] * member_cols
    send_grads = (out_grad.astype(jnp.float32)[None] * weight_cols).astype(jnp.bfloat16)
    got_rows, got_grads = (
        lax.all_to_all(send_rows, "expert", split_axis=0, concat_axis=0, tiled=True),
        lax.all_to_all(send_grads, "expert", split_axis=0, concat_axis=0, tiled=True),
    )
    rows_in, grads_in = (
        lax.all_gather(got_rows.reshape(total_rows, feat_width), "tensor", axis=1, tiled=True),
        lax.all_gather(got_grads.reshape(total_rows, feat_width), "tensor", axis=1, tiled=True),
    )
    gate_all, up_all, down_all = (
        lax.all_to_all(w_gate, "tensor", split_axis=2, concat_axis=1, tiled=True),
        lax.all_to_all(w_up, "tensor", split_axis=2, concat_axis=1, tiled=True),
        lax.all_to_all(w_down, "tensor", split_axis=2, concat_axis=1, tiled=True),
    )
    gate_w = gate_all[0]
    up_w = up_all[0]
    down_w = down_all[0]
    gate_pre = jnp.dot(rows_in, gate_w, preferred_element_type=jnp.float32) * gate_scale[0]
    up_pre = jnp.dot(rows_in, up_w, preferred_element_type=jnp.float32) * up_scale[0]
    sigma = jax.nn.sigmoid(gate_pre)
    active = gate_pre * sigma
    hidden = (active * up_pre * down_scale[0]).astype(jnp.bfloat16)
    out_part = jnp.dot(hidden, down_w.T, preferred_element_type=jnp.float32)
    down_grad = contract_rows(grads_in, hidden).astype(jnp.bfloat16)
    back = jnp.dot(grads_in, down_w, preferred_element_type=jnp.float32) * down_scale[0]
    d_gate = (back * up_pre * sigma * (1.0 + gate_pre * (1.0 - sigma)) * gate_scale[0]).astype(
        jnp.bfloat16
    )
    d_up = (back * active * up_scale[0]).astype(jnp.bfloat16)
    gate_grad = contract_rows(rows_in, d_gate).astype(jnp.bfloat16)
    up_grad = contract_rows(rows_in, d_up).astype(jnp.bfloat16)
    grad_part = jnp.dot(d_gate, gate_w.T, preferred_element_type=jnp.float32) + jnp.dot(
        d_up, up_w.T, preferred_element_type=jnp.float32
    )
    out_sum = lax.psum_scatter(
        out_part.astype(jnp.bfloat16), "tensor", scatter_dimension=1, tiled=True
    )
    out_back = lax.all_to_all(
        out_sum.reshape(groups, local_tokens, feat_width),
        "expert",
        split_axis=0,
        concat_axis=0,
        tiled=True,
    )
    grad_sum = lax.psum_scatter(
        grad_part.astype(jnp.bfloat16), "tensor", scatter_dimension=1, tiled=True
    )
    grad_back = lax.all_to_all(
        grad_sum.reshape(groups, local_tokens, feat_width),
        "expert",
        split_axis=0,
        concat_axis=0,
        tiled=True,
    )
    out_float = unpacking(out_back)
    grad_float = unpacking(grad_back)
    mixed = jnp.sum(weight_cols * out_float, axis=0).astype(jnp.bfloat16)
    token_grad = jnp.sum(grad_float, axis=0).astype(jnp.bfloat16)
    local_score = jnp.einsum("td,etd->te", out_grad.astype(jnp.float32), out_float)
    score = lax.psum(local_score, "tensor")
    pick = jnp.sum(chosen * score[:, None, :], axis=2)
    mean_pick = jnp.sum(probs * pick, axis=1, keepdims=True)
    logit_grad = probs * (pick - mean_pick)
    return (mixed, token_grad, logit_grad, gate_grad[None], up_grad[None], down_grad[None])


def solution(mesh):
    in_specs = (
        P("expert", "tensor"),
        P("expert", "tensor"),
        P("expert", None),
        P("expert", None),
        P("expert", "tensor", None),
        P("expert", "tensor", None),
        P("expert", "tensor", None),
        P("expert", "tensor"),
        P("expert", "tensor"),
        P("expert", "tensor"),
    )
    out_specs = (
        P("expert", "tensor"),
        P("expert", "tensor"),
        P("expert", None),
        P("expert", None, "tensor"),
        P("expert", None, "tensor"),
        P("expert", None, "tensor"),
    )
    return jax.shard_map(body, mesh=mesh, in_specs=in_specs, out_specs=out_specs, check_vma=False)
```

profile of v0, /device:TPU:0, one launch (start us, length us, event | category | flops | bytes accessed | tf_op | source)
XLA Modules:
  0.0 1169.9 jit_solution(9757918283287078089)
XLA Ops:
  7.2 0.7 convert_reduce_fusion
  7.9 1.9 broadcast_multiply_fusion
  9.8 6.3 all-to-all-start
  16.1 51.2 %copy.36 = bf16[1,768,8192]{1,0,2:T(2,128)(2,1)} copy(bf16[1,768,8192]{2,1,0:T(8,128)(2,1)} %param.14) | data formatting | bytes 25165824 | tf_op args[4]
  67.4 0.5 broadcast.37
  67.9 126.8 %reduce.1 = bf16[8192,768]{1,0:T(8,128)(2,1)} reduce(bf16[8192,1,768]{2,1,0:T(2,128)(2,1)} %bitcast.55, bf16[]{:T(256)} %broadcast.37), dimensions={1}, to_apply=%bitcast.33.reduce_sub_computation | reduce | bytes 25165826
  194.7 12.3 %reshape.43 = bf16[8,2,393216]{2,1,0:T(2,128)(2,1)} reshape(bf16[8192,768]{1,0:T(8,128)(2,1)} %reduce.1) | data formatting | bytes 25165824
  207.0 0.0 all-to-all-done
  207.0 0.9 copy-done
  207.9 5.9 all-to-all-start.1
  213.8 51.2 %copy.38 = bf16[1,768,8192]{1,0,2:T(2,128)(2,1)} copy(bf16[1,768,8192]{2,1,0:T(8,128)(2,1)} %param.15) | data formatting | bytes 25165824 | tf_op args[5]
  265.0 126.8 %reduce.2 = bf16[8192,768]{1,0:T(8,128)(2,1)} reduce(bf16[8192,1,768]{2,1,0:T(2,128)(2,1)} %bitcast.60, bf16[]{:T(256)} %broadcast.37), dimensions={1}, to_apply=%bitcast.31.reduce_sub_computation | reduce | bytes 25165826
  391.8 12.3 %reshape.41 = bf16[8,2,393216]{2,1,0:T(2,128)(2,1)} reshape(bf16[8192,768]{1,0:T(8,128)(2,1)} %reduce.2) | data formatting | bytes 25165824
  404.1 0.0 all-to-all-done.1
  404.1 5.5 all-to-all-start.2
  409.6 51.2 %copy.40 = bf16[1,768,8192]{1,0,2:T(2,128)(2,1)} copy(bf16[1,768,8192]{2,1,0:T(8,128)(2,1)} %param.16) | data formatting | bytes 25165824 | tf_op args[6]
  460.8 126.8 %reduce.3 = bf16[8192,768]{1,0:T(8,128)(2,1)} reduce(bf16[8192,1,768]{2,1,0:T(2,128)(2,1)} %bitcast.56, bf16[]{:T(256)} %broadcast.37), dimensions={1}, to_apply=%bitcast.35.reduce_sub_computation | reduce | bytes 25165826
  587.6 12.3 %reshape.45 = bf16[8,2,393216]{2,1,0:T(2,128)(2,1)} reshape(bf16[8192,768]{1,0:T(8,128)(2,1)} %reduce.3) | data formatting | bytes 25165824
  599.9 0.0 all-to-all-done.2
  599.9 5.3 all-to-all-start.3
  605.2 0.0 all-gather.3.cloned.1.call-start
  605.3 0.7 all-gather.3.cloned.1.call-update
  606.0 0.3 reduce-scatter.3.cloned.1.call-start
  606.2 18.0 %reshape.44 = bf16[8192,1,768]{2,1,0:T(2,128)(2,1)} reshape(bf16[8,2,393216]{2,1,0:T(2,128)(2,1)} %all-to-all-done.1) | data formatting | bytes 25165824
  624.2 15.1 %copy.45 = bf16[1,768,8192]{1,2,0:T(8,128)(2,1)} copy(bf16[1,768,8192]{1,0,2:T(2,128)(2,1)} %bitcast.57) | data formatting | bytes 25165824
  639.3 16.6 %copy.37 = bf16[1,8,768,1024]{3,2,1,0:T(8,128)(2,1)} copy(bf16[1,8,768,1024]{2,3,1,0:T(8,128)(2,1)} %bitcast.61) | data formatting | bytes 25165824 | tf_op jit(solution)/shard_map/all_to_all | solution.py:56
  655.9 18.1 %reshape.42 = bf16[8192,1,768]{2,1,0:T(2,128)(2,1)} reshape(bf16[8,2,393216]{2,1,0:T(2,128)(2,1)} %all-to-all-done.2) | data formatting | bytes 25165824
  673.9 15.1 %copy.46 = bf16[1,768,8192]{1,2,0:T(8,128)(2,1)} copy(bf16[1,768,8192]{1,0,2:T(2,128)(2,1)} %bitcast.58) | data formatting | bytes 25165824
  689.0 16.6 %copy.39 = bf16[1,8,768,1024]{3,2,1,0:T(8,128)(2,1)} copy(bf16[1,8,768,1024]{2,3,1,0:T(8,128)(2,1)} %bitcast.62) | data formatting | bytes 25165824 | tf_op jit(solution)/shard_map/all_to_all | solution.py:57
  705.6 63.9 %all-to-all-done.3 = bf16[8,2,393216]{2,1,0:T(2,128)(2,1)} async-done(((bf16[8,2,393216]{2,1,0:T(2,128)(2,1)}), bf16[8,2,393216]{2,1,0:T(2,128)(2,1)}, u32[]{:S(2)}, u32[]{:S(2)}) %all-to-all-start.3) | async-done | bytes 12582944 | tf_op jit(solution)/shard_map/all_to_all | solution.py:58
  769.5 17.9 %reshape.46 = bf16[8192,1,768]{2,1,0:T(2,128)(2,1)} reshape(bf16[8,2,393216]{2,1,0:T(2,128)(2,1)} %all-to-all-done.3) | data formatting | bytes 25165824
  787.5 15.1 %copy.47 = bf16[1,768,8192]{1,2,0:T(8,128)(2,1)} copy(bf16[1,768,8192]{1,0,2:T(2,128)(2,1)} %bitcast.59) | data formatting | bytes 25165824
  802.5 16.6 %copy.41 = bf16[1,8,768,1024]{3,2,1,0:T(8,128)(2,1)} copy(bf16[1,8,768,1024]{2,3,1,0:T(8,128)(2,1)} %bitcast.63) | data formatting | bytes 25165824 | tf_op jit(solution)/shard_map/all_to_all | solution.py:58
  819.2 0.0 copy-start.7
  819.2 0.0 slice-start
  819.2 0.0 slice-start.1
  819.2 13.3 %fusion.4 = f32[512,1024]{1,0:T(8,128)S(1)} fusion(bf16[512,6144]{1,0:T(8,128)(2,1)} %all-gather.3.cloned.1.call-done, bf16[6144,1024]{1,0:T(8,128)(2,1)} %bitcast.64), kind=kOutput, calls=%fused_computation.26 | convolution fusion | flops 6442450944 | bytes 20971520 | tf_op jit(solution)/shard_map/dot_general | solution.py:63
  832.6 11.8 %multiply_convert_fusion.2 = (bf16[512,1024]{1,0:T(8,128)(2,1)S(1)}, f32[512,1024]{1,0:T(8,128)}) fusion(f32[1024]{0:T(1024)S(1)} %bitcast.82, f32[1024]{0:T(1024)S(1)} %bitcast.84, f32[512,1024]{1,0:T(8,128)S(1)} %fusion.4, f32[1024]{0:T(1024)S(1)} %bitcast.86, bf16[512,6144]{1,0:T(8,128)(2,1)S(1)} %copy-done.4, bf16[6144,1024]{1,0:T(8,128)(2,1)} %bitcast.66), kind=kOutput, calls=%fused_computation.7 | convolution fusion | flops 6447169536 | bytes 24129536 | tf_op jit(solution)/shard_map/dot_general | solution.py:64
  844.4 1.0 copy-done.10
  845.4 8.6 convolution_convert_fusion
  854.0 0.0 reduce-scatter.3.cloned.1.call-update
  854.0 61.4 %reduce-scatter.3.cloned.1.call-done = bf16[512,768]{1,0:T(8,128)(2,1)} async-done(((bf16[512,6144]{1,0:T(8,128)(2,1)}), bf16[512,768]{1,0:T(8,128)(2,1)}) %reduce-scatter.3.cloned.1.call-update) | async-done | bytes 786448 | tf_op jit(solution)/shard_map/reduce_scatter | solution.py:80
  915.4 4.6 all-to-all-start.4
  920.1 19.9 %all-to-all-done.4 = bf16[4,128,768]{2,1,0:T(8,128)(2,1)S(1)} async-done(((bf16[4,128,768]{2,1,0:T(8,128)(2,1)}), bf16[4,128,768]{2,1,0:T(8,128)(2,1)S(1)}, u32[]{:S(2)}, u32[]{:S(2)}) %all-to-all-start.4) | async-done | bytes 786464 | tf_op jit(solution)/shard_map/all_to_all | solution.py:83
  940.0 1.0 fusion.1
  941.0 0.1 copy.44
  941.1 12.0 %psum.7 = f32[128,4]{0,1:T(4,128)S(1)} all-reduce(f32[128,4]{0,1:T(4,128)S(1)} %bitcast.78), channel_id=1, replica_groups=mesh['expert'=4,'tensor'=8] {'tensor'}, use_global_device_ids=true, to_apply=%region_6.0 | all-reduce | flops 512 | bytes 4096 | tf_op jit(solution)/shard_map/psum | solution.py:105
  953.1 1.0 multiply_convert_fusion.3
  954.0 23.3 %all_to_all.65 = bf16[4,128,768]{2,1,0:T(8,128)(2,1)} all-to-all(bf16[4,128,768]{2,1,0:T(8,128)(2,1)S(1)} %get-tuple-element.12), channel_id=1, replica_groups=mesh['expert'=4,'tensor'=8] {'expert'}, dimensions={0} | all-to-all | bytes 1572864 | tf_op jit(solution)/shard_map/all_to_all | solution.py:49
  977.4 0.0 all-gather.5.cloned.1.call-update
  977.4 0.0 reduce-scatter.5.cloned.1.call-start
  977.5 43.5 %all-gather.5.cloned.1.call-done = bf16[512,6144]{1,0:T(8,128)(2,1)} async-done(((bf16[512,768]{1,0:T(8,128)(2,1)}), bf16[512,6144]{1,0:T(8,128)(2,1)}) %all-gather.5.cloned.1.call-update) | async-done | bytes 6291472 | tf_op jit(solution)/shard_map/all_gather | solution.py:53
  1021.0 14.6 %multiply_convert_fusion = (bf16[512,1024]{1,0:T(8,128)(2,1)S(1)}, bf16[512,1024]{1,0:T(8,128)(2,1)S(1)}) fusion(f32[1024]{0:T(1024)S(1)} %bitcast.83, f32[1024]{0:T(1024)S(1)} %bitcast.85, f32[512,1024]{1,0:T(8,128)} %copy-done.12, f32[1024]{0:T(1024)S(1)} %bitcast.87, f32[512,1024]{1,0:T(8,128)} %get-tuple-element.15, ...), kind=kOutput, calls=%fused_computation.5 | convolution fusion | flops 6451888128 | bytes 25178112 | tf_op jit(solution)/shard_map/dot_general | solution.py:70
  1035.6 20.2 %fusion.5 = f32[512,6144]{1,0:T(8,128)} fusion(bf16[512,1024]{1,0:T(8,128)(2,1)S(1)} %get-tuple-element.11, bf16[6144,1024]{1,0:T(8,128)(2,1)} %bitcast.65), kind=kOutput, calls=%fused_computation.27 | convolution fusion | flops 6442450944 | bytes 26214400 | tf_op jit(solution)/shard_map/dot_general | solution.py:77
  1055.8 20.3 %add_convert_fusion = bf16[512,6144]{1,0:T(8,128)(2,1)} fusion(f32[512,6144]{1,0:T(8,128)} %fusion.5, bf16[512,1024]{1,0:T(8,128)(2,1)S(1)} %get-tuple-element.10, bf16[6144,1024]{1,0:T(8,128)(2,1)} %bitcast.67), kind=kOutput, calls=%fused_computation.3 | convolution fusion | flops 6448742400 | bytes 32505856 | tf_op jit(solution)/shard_map/dot_general | solution.py:77
  1076.1 0.0 reduce-scatter.5.cloned.1.call-update
  1076.1 0.6 subtract_multiply_fusion
  1076.7 12.5 %convert_bitcast_fusion.1 = bf16[1,6144,1024]{2,1,0:T(8,128)(2,1)} fusion(bf16[512,6144]{1,0:T(8,128)(2,1)} %all-gather.3.cloned.1.call-done, bf16[512,1024]{1,0:T(8,128)(2,1)} %copy-done.11), kind=kOutput, calls=%fused_computation.1 | convolution fusion | flops 6448742400 | bytes 19922944 | tf_op jit(solution)/shard_map/dot_general | solution.py:18
  1089.2 9.8 convert_bitcast_fusion.2
  1099.0 38.8 %reduce-scatter.5.cloned.1.call-done = bf16[512,768]{1,0:T(8,128)(2,1)} async-done(((bf16[512,6144]{1,0:T(8,128)(2,1)}), bf16[512,768]{1,0:T(8,128)(2,1)}) %reduce-scatter.5.cloned.1.call-update) | async-done | bytes 786448 | tf_op jit(solution)/shard_map/reduce_scatter | solution.py:90
  1137.9 4.6 all-to-all-start.6
  1142.5 11.8 %convert_bitcast_fusion = bf16[1,6144,1024]{2,1,0:T(8,128)(2,1)} fusion(bf16[512,6144]{1,0:T(8,128)(2,1)} %all-gather.5.cloned.1.call-done, bf16[512,1024]{1,0:T(8,128)(2,1)} %copy-done.10), kind=kOutput, calls=%fused_computation | convolution fusion | flops 6448742400 | bytes 19922944 | tf_op jit(solution)/shard_map/dot_general | solution.py:18
  1154.3 8.1 all-to-all-done.6
  1162.4 0.8 reduce_sum.60
  (40 shorter events, 0.2 us)
Async XLA Ops:
  9.8 197.2 %all-to-all-start = ((bf16[4,128,768]{2,1,0:T(8,128)(2,1)}), bf16[4,128,768]{2,1,0:T(8,128)(2,1)S(1)}, u32[]{:S(2)}, u32[]{:S(2)}) async-start(bf16[4,128,768]{2,1,0:T(8,128)(2,1)} %broadcast_multiply_fusion), calls=%async_computation | async-start | bytes 1572864 | tf_op jit(solution)/shard_map/all_to_all | solution.py:48
  207.0 0.9 copy-start
  207.9 196.2 %all-to-all-start.1 = ((bf16[8,2,393216]{2,1,0:T(2,128)(2,1)}), bf16[8,2,393216]{2,1,0:T(2,128)(2,1)}, u32[]{:S(2)}, u32[]{:S(2)}) async-start(bf16[8,2,393216]{2,1,0:T(2,128)(2,1)} %reshape.43), calls=%async_computation.1 | async-start | bytes 25165824 | tf_op jit(solution)/shard_map/all_to_all | solution.py:56
  404.1 195.8 %all-to-all-start.2 = ((bf16[8,2,393216]{2,1,0:T(2,128)(2,1)}), bf16[8,2,393216]{2,1,0:T(2,128)(2,1)}, u32[]{:S(2)}, u32[]{:S(2)}) async-start(bf16[8,2,393216]{2,1,0:T(2,128)(2,1)} %reshape.41), calls=%async_computation.2 | async-start | bytes 25165824 | tf_op jit(solution)/shard_map/all_to_all | solution.py:57
  599.9 169.6 %all-to-all-start.3 = ((bf16[8,2,393216]{2,1,0:T(2,128)(2,1)}), bf16[8,2,393216]{2,1,0:T(2,128)(2,1)}, u32[]{:S(2)}, u32[]{:S(2)}) async-start(bf16[8,2,393216]{2,1,0:T(2,128)(2,1)} %reshape.45), calls=%async_computation.3 | async-start | bytes 25165824 | tf_op jit(solution)/shard_map/all_to_all | solution.py:58
  605.2 213.9 %all-gather.3.cloned.1.call-start = ((), (), s32[]{:S(2)}) async-start(), calls=%async_computation.9 | async-start | bytes 7077888 | tf_op jit(solution)/shard_map/all_gather | solution.py:52
  606.0 309.4 %reduce-scatter.3.cloned.1.call-start = ((), (), s32[]{:S(2)}) async-start(), calls=%async_computation.10 | async-start | bytes 7077888 | tf_op jit(solution)/shard_map/reduce_scatter | solution.py:80
  819.2 13.4 %copy-start.4 = (bf16[512,6144]{1,0:T(8,128)(2,1)S(1)}, bf16[512,6144]{1,0:T(8,128)(2,1)}, u32[]{:S(2)}) copy-start(bf16[512,6144]{1,0:T(8,128)(2,1)} %all-gather.3.cloned.1.call-done) | copy-start | bytes 18874372
  819.2 13.4 %copy-start.5 = (f32[1,1024]{1,0:T(1,128)S(1)}, f32[1,1024]{1,0:T(1,128)}, u32[]{:S(2)}) copy-start(f32[1,1024]{1,0:T(1,128)} %param.19) | copy-start | bytes 12292
  819.2 13.4 %copy-start.6 = (f32[1,1024]{1,0:T(1,128)S(1)}, f32[1,1024]{1,0:T(1,128)}, u32[]{:S(2)}) copy-start(f32[1,1024]{1,0:T(1,128)} %param.18) | copy-start | bytes 12292
  819.2 13.4 %copy-start.7 = (f32[1,1024]{1,0:T(1,128)S(1)}, f32[1,1024]{1,0:T(1,128)}, u32[]{:S(2)}) copy-start(f32[1,1024]{1,0:T(1,128)} %param.17) | copy-start | bytes 12292
  819.2 26.2 %slice-start = ((s8[12582912]{0:T(1024)(128)(4,1)}), s8[4194304]{0:T(1024)(128)(4,1)S(1)}, s32[]{:S(2)}) async-start(s8[12582912]{0:T(1024)(128)(4,1)} %bitcast.69), calls=%async_computation.13 | async-start | bytes 8388608
  819.2 26.2 %slice-start.1 = ((s8[12582912]{0:T(1024)(128)(4,1)}), s8[4194304]{0:T(1024)(128)(4,1)S(1)}, s32[]{:S(2)}) async-start(s8[12582912]{0:T(1024)(128)(4,1)} %bitcast.69), calls=%async_computation.14 | async-start | bytes 8388608
  832.5 11.8 %copy-start.12 = (f32[512,1024]{1,0:T(8,128)}, f32[512,1024]{1,0:T(8,128)S(1)}, u32[]{:S(2)}) copy-start(f32[512,1024]{1,0:T(8,128)S(1)} %fusion.4) | copy-start | bytes 6291460
  832.6 12.8 %slice-start.2 = ((s8[12582912]{0:T(1024)(128)(4,1)}), s8[4194304]{0:T(1024)(128)(4,1)S(1)}, s32[]{:S(2)}) async-start(s8[12582912]{0:T(1024)(128)(4,1)} %bitcast.69), calls=%async_computation.15 | async-start | bytes 8388608
  844.4 1.0 copy-start.10
  854.0 66.0 %copy-start.1 = (bf16[128,768]{1,0:T(8,128)(2,1)S(1)}, bf16[128,768]{1,0:T(8,128)(2,1)}, u32[]{:S(2)}) copy-start(bf16[128,768]{1,0:T(8,128)(2,1)} %param.11) | copy-start | bytes 589828
  854.0 66.1 %copy-start.3 = (f32[128,2]{0,1:T(2,128)S(1)}, f32[128,2]{0,1:T(2,128)}, u32[]{:S(2)}) copy-start(f32[128,2]{0,1:T(2,128)} %param.13) | copy-start | bytes 3076
  854.0 99.0 %copy-start.2 = (s32[128,2]{0,1:T(2,128)S(1)}, s32[128,2]{0,1:T(2,128)}, u32[]{:S(2)}) copy-start(s32[128,2]{0,1:T(2,128)} %param.12) | copy-start | bytes 3076
  915.4 24.6 %all-to-all-start.4 = ((bf16[4,128,768]{2,1,0:T(8,128)(2,1)}), bf16[4,128,768]{2,1,0:T(8,128)(2,1)S(1)}, u32[]{:S(2)}, u32[]{:S(2)}) async-start(bf16[4,128,768]{2,1,0:T(8,128)(2,1)} %bitcast.75), calls=%async_computation.5 | async-start | bytes 1572864 | tf_op jit(solution)/shard_map/all_to_all | solution.py:83
  920.0 100.9 %all-gather.5.cloned.1.call-start = ((), (), s32[]{:S(2)}) async-start(), calls=%async_computation.11 | async-start | bytes 7077888 | tf_op jit(solution)/shard_map/all_gather | solution.py:53
  977.4 160.4 %reduce-scatter.5.cloned.1.call-start = ((), (), s32[]{:S(2)}) async-start(), calls=%async_computation.12 | async-start | bytes 7077888 | tf_op jit(solution)/shard_map/reduce_scatter | solution.py:90
  1035.6 20.2 %copy-start.8 = (bf16[512,1024]{1,0:T(8,128)(2,1)}, bf16[512,1024]{1,0:T(8,128)(2,1)S(1)}, u32[]{:S(2)}) copy-start(bf16[512,1024]{1,0:T(8,128)(2,1)S(1)} %get-tuple-element.11) | copy-start | bytes 3145732
  1035.6 20.2 %copy-start.11 = (bf16[512,1024]{1,0:T(8,128)(2,1)}, bf16[512,1024]{1,0:T(8,128)(2,1)S(1)}, u32[]{:S(2)}) copy-start(bf16[512,1024]{1,0:T(8,128)(2,1)S(1)} %get-tuple-element.10) | copy-start | bytes 3145732
  1076.0 13.2 %slice-start.3 = ((s8[6291456]{0:T(1024)(128)(4,1)}), s8[2097152]{0:T(1024)(128)(4,1)S(1)}, s32[]{:S(2)}) async-start(s8[6291456]{0:T(1024)(128)(4,1)} %bitcast.80), calls=%async_computation.16 | async-start | bytes 4194304
  1076.7 12.5 %slice-start.4 = ((s8[6291456]{0:T(1024)(128)(4,1)}), s8[4194304]{0:T(1024)(128)(4,1)S(1)}, s32[]{:S(2)}) async-start(s8[6291456]{0:T(1024)(128)(4,1)} %bitcast.80), calls=%async_computation.17 | async-start | bytes 8388608
  1076.7 12.5 %copy-start.9 = (bf16[512,1024]{1,0:T(8,128)(2,1)S(1)}, bf16[512,1024]{1,0:T(8,128)(2,1)}, u32[]{:S(2)}) copy-start(bf16[512,1024]{1,0:T(8,128)(2,1)} %copy-done.8) | copy-start | bytes 3145732
  1137.9 24.5 %all-to-all-start.6 = ((bf16[4,128,768]{2,1,0:T(8,128)(2,1)}), bf16[4,128,768]{2,1,0:T(8,128)(2,1)S(1)}, u32[]{:S(2)}, u32[]{:S(2)}) async-start(bf16[4,128,768]{2,1,0:T(8,128)(2,1)} %bitcast.74), calls=%async_computation.8 | async-start | bytes 1572864 | tf_op jit(solution)/shard_map/all_to_all | solution.py:93
Sparse Core Ops, SparseCore 0:
  608.0 112.5 all-gather.2
  854.1 61.2 reduce-scatter.2
  977.5 43.3 all-gather.4
  1076.2 61.6 reduce-scatter.4
where the time goes:
time: 1180 us; the launch traced here: 1170 us
  other arithmetic  385 us (33%)
  local copies, waits for them, and re-layouts  342 us (29%)
  waiting for transfers between devices  236 us (20%)
  matrix products  124 us (11%)
  blocking collectives  35.3 us (3%)
  starting transfers between devices  32.6 us (3%)
  between operations  14.1 us (1%)
    unnamed x5, other arithmetic  380 us
    unnamed x49, local copies, waits for them, and re-layouts  292 us
    all_to_all x1, waiting for transfers between devices, body(): lax.all_to_all(w_down, 'tensor', split_axis=2, concat_axis=1, tiled=True)  63.9 us
    reduce_scatter x1, waiting for transfers between devices, body(): lax.psum_scatter(out_part.astype(jnp.bfloat16), 'tensor', scatter_dimensi...  61.4 us
    all_gather x1, waiting for transfers between devices, body(): lax.all_gather(got_grads.reshape(total_rows, feat_width), 'tensor', axis=...  43.5 us
    reduce_scatter x1, waiting for transfers between devices, body(): lax.psum_scatter(grad_part.astype(jnp.bfloat16), 'tensor', scatter_dimens...  38.8 us
    dot_general x3, matrix products, contract_rows(): lax.dot_general(left, right, (((0,), (0,)), ((), ())), preferred_element_...  34.2 us
  transfers between devices with their start and end apart: 10, of which 6 were waited for; matrix products, arithmetic and copies ran while one was open for 65% of the time, Pallas kernels for 0%

commit v1 on v0

v1 whole, which is shorter than its diff:
```python
import jax
import jax.numpy as jnp
from jax import lax
from jax.sharding import PartitionSpec as P


def gate_tables(expert_ids, route_logits, count):
    first = jax.nn.sigmoid(route_logits[:, 0] - route_logits[:, 1])
    probs = jnp.stack([first, 1.0 - first], axis=1)
    labels = jnp.arange(count, dtype=jnp.int32)
    chosen = (expert_ids[:, :, None] == labels[None, None, :]).astype(jnp.float32)
    per_expert = jnp.sum(probs[:, :, None] * chosen, axis=1)
    member = jnp.sum(chosen, axis=1)
    return (probs, chosen, per_expert, member)


def contract_rows(left, right):
    return lax.dot_general(
        left, right, (((0,), (0,)), ((), ())), preferred_element_type=jnp.float32
    )


def body(
    tokens,
    out_grad,
    expert_ids,
    route_logits,
    w_gate,
    w_up,
    w_down,
    gate_scale,
    up_scale,
    down_scale,
):
    groups = lax.axis_size("expert")
    local_tokens, feat_width = tokens.shape
    cap = local_tokens * 5 // 8
    total_rows = groups * cap
    probs, chosen, per_expert, member = gate_tables(expert_ids, route_logits, groups)
    weight_cols = per_expert.T[:, :, None]
    earlier = jnp.tril(jnp.ones((local_tokens, local_tokens), jnp.bfloat16), -1)
    rank = jnp.dot(earlier, member.astype(jnp.bfloat16), preferred_element_type=jnp.float32)
    slots = jnp.arange(cap, dtype=jnp.float32)
    place = jnp.where(
        (member.T[:, None, :] > 0) & (rank.T[:, None, :] == slots[None, :, None]), 1.0, 0.0
    ).astype(jnp.bfloat16)

    weighted = (out_grad.astype(jnp.float32)[None] * weight_cols).astype(jnp.bfloat16)
    send_rows = jnp.einsum("eit,td->eid", place, tokens, preferred_element_type=jnp.float32)
    send_grads = jnp.einsum("eit,etd->eid", place, weighted, preferred_element_type=jnp.float32)
    send = jnp.stack([send_rows, send_grads], axis=1).astype(jnp.bfloat16)
    got = lax.all_to_all(send, "expert", split_axis=0, concat_axis=0, tiled=True)
    rows_loc = got[:, 0].reshape(total_rows, feat_width)
    grads_loc = got[:, 1].reshape(total_rows, feat_width)
    gate_w, up_w, down_w = w_gate[0], w_up[0], w_down[0]

    def project(left, right):
        part = jnp.dot(left, right, preferred_element_type=jnp.float32).astype(jnp.bfloat16)
        full = lax.psum_scatter(part, "tensor", scatter_dimension=1, tiled=True)
        return full.astype(jnp.float32)

    def gather(value):
        return lax.all_gather(value, "tensor", axis=1, tiled=True)

    def back_project(left, right):
        return lax.dot_general(
            left, right, (((1,), (1,)), ((), ())), preferred_element_type=jnp.float32
        )

    def send_back(value):
        return lax.all_to_all(
            value.astype(jnp.bfloat16).reshape(groups, cap, feat_width),
            "expert",
            split_axis=0,
            concat_axis=0,
            tiled=True,
        )

    gate_pre = project(rows_loc, gate_w) * gate_scale[0]
    up_pre = project(rows_loc, up_w) * up_scale[0]
    back = project(grads_loc, down_w) * down_scale[0]
    rows_in = gather(rows_loc)
    grads_in = gather(grads_loc)
    sigma = jax.nn.sigmoid(gate_pre)
    active = gate_pre * sigma
    hidden = (active * up_pre * down_scale[0]).astype(jnp.bfloat16)
    d_gate = (back * up_pre * sigma * (1.0 + gate_pre * (1.0 - sigma)) * gate_scale[0]).astype(
        jnp.bfloat16
    )
    d_up = (back * active * up_scale[0]).astype(jnp.bfloat16)
    out_back = send_back(back_project(gather(hidden), down_w))
    grad_back = send_back(
        back_project(gather(d_gate), gate_w) + back_project(gather(d_up), up_w)
    )
    down_grad = contract_rows(grads_in, hidden).astype(jnp.bfloat16)
    gate_grad = contract_rows(rows_in, d_gate).astype(jnp.bfloat16)
    up_grad = contract_rows(rows_in, d_up).astype(jnp.bfloat16)
    out_float = jnp.einsum("eit,eid->etd", place, out_back, preferred_element_type=jnp.float32)
    token_grad = lax.dot_general(
        place.reshape(total_rows, local_tokens),
        grad_back.reshape(total_rows, feat_width),
        (((0,), (0,)), ((), ())),
        preferred_element_type=jnp.float32,
    ).astype(jnp.bfloat16)
    mixed = jnp.sum(weight_cols * out_float, axis=0).astype(jnp.bfloat16)
    local_score = jnp.einsum("td,etd->te", out_grad.astype(jnp.float32), out_float)
    score = lax.psum(local_score, "tensor")
    pick = jnp.sum(chosen * score[:, None, :], axis=2)
    mean_pick = jnp.sum(probs * pick, axis=1, keepdims=True)
    logit_grad = probs * (pick - mean_pick)
    return (mixed, token_grad, logit_grad, gate_grad[None], up_grad[None], down_grad[None])


def solution(mesh):
    in_specs = (
        P("expert", "tensor"),
        P("expert", "tensor"),
        P("expert", None),
        P("expert", None),
        P("expert", "tensor", None),
        P("expert", "tensor", None),
        P("expert", "tensor", None),
        P("expert", "tensor"),
        P("expert", "tensor"),
        P("expert", "tensor"),
    )
    out_specs = (
        P("expert", "tensor"),
        P("expert", "tensor"),
        P("expert", None),
        P("expert", None, "tensor"),
        P("expert", None, "tensor"),
        P("expert", None, "tensor"),
    )
    return jax.shard_map(body, mesh=mesh, in_specs=in_specs, out_specs=out_specs, check_vma=False)
```

time: 1180 us -> 472 us (0.40)
  other arithmetic: 385 us -> 6.8 us
  local copies, waits for them, and re-layouts: 342 us -> 0.25 us
  waiting for transfers between devices: 236 us -> 295 us
  starting transfers between devices: 32.6 us -> 9.82 us
  matrix products: 124 us -> 102 us
    unnamed x5 -> x0, other arithmetic: 380 us -> none
    unnamed x49 -> x24, local copies, waits for them, and re-layouts: 292 us -> 0.06 us
    all_gather x2 -> x5, waiting for transfers between devices: 43.5 us -> 139 us  [gather(): return lax.all_gather(value, 'tensor', axis=1, tiled=True)]
    all_to_all x6 -> x2, waiting for transfers between devices: 91.8 us -> 0.01 us  [send_back(): lax.all_to_all(value.astype(jnp.bfloat16).reshape(groups, cap, feat_width...]
    reduce_scatter x2 -> x3, waiting for transfers between devices: 100 us -> 153 us  [project(): full = lax.psum_scatter(part, 'tensor', scatter_dimension=1, tiled=True)]
    all_to_all x3 -> x0, local copies, waits for them, and re-layouts: 49.9 us -> none  [the longest x1 16.6 us: body(): lax.all_to_all(w_down, 'tensor', split_axis=2, concat_axis=1, tiled=True)]
    all_to_all x6 -> x2, starting transfers between devices: 32.3 us -> 9.32 us  [send_back(): lax.all_to_all(value.astype(jnp.bfloat16).reshape(groups, cap, feat_width...]
    dot_general x6 -> x11, matrix products: 88.8 us -> 67.3 us  [the longest x3 32.8 us: project(): jnp.dot(left, right, preferred_element_type=jnp.float32)]
  transfers between devices with their start and end apart: 10 -> 10, of which waited for: 6 -> 8; matrix products, arithmetic and copies ran while one was open for 65% -> 20% of each run, Pallas kernels for 0% -> 0%
where the time goes in v1:
time: 472 us
  waiting for transfers between devices  295 us (62%)
  matrix products  102 us (22%)
  blocking collectives  43.9 us (9%)
  between operations  14.3 us (3%)
  starting transfers between devices  9.82 us (2%)
  other arithmetic  6.8 us (1%)
    reduce_scatter x3, waiting for transfers between devices, project(): full = lax.psum_scatter(part, 'tensor', scatter_dimension=1, tiled=True)  153 us
    all_gather x5, waiting for transfers between devices, gather(): return lax.all_gather(value, 'tensor', axis=1, tiled=True)  139 us
    dot_general x3, matrix products, contract_rows(): lax.dot_general(left, right, (((0,), (0,)), ((), ())), preferred_element_...  33.6 us
    dot_general x3, matrix products, project(): jnp.dot(left, right, preferred_element_type=jnp.float32)  32.8 us
    dot_general x3, matrix products, back_project(): lax.dot_general(left, right, (((1,), (1,)), ((), ())), preferred_element_...  31.6 us
    all_to_all x1, blocking collectives, body(): lax.all_to_all(send, 'expert', split_axis=0, concat_axis=0, tiled=True)  30.5 us
    psum x1, blocking collectives, body(): score = lax.psum(local_score, 'tensor')  13.4 us
  transfers between devices with their start and end apart: 10, of which 8 were waited for; matrix products, arithmetic and copies ran while one was open for 20% of the time, Pallas kernels for 0%

profile of v1, /device:TPU:0, one launch (start us, length us, event | category | flops | bytes accessed | tf_op | source)
XLA Modules:
  0.0 471.8 jit_solution(13692234341856689508)
XLA Ops:
  7.2 0.0 copy-start
  7.2 0.0 reduce-scatter.8.cloned.1.call-start
  7.2 0.8 broadcast_subtract_fusion
  8.0 0.7 convert_reduce_fusion
  8.7 0.2 fusion.59
  8.9 1.0 convert_element_type.68
  9.9 0.0 copy-done
  9.9 0.3 fusion.33
  10.2 0.4 fusion.34
  10.6 0.1 pad_maximum_fusion
  10.7 0.1 copy.21
  10.7 30.5 %all_to_all.15 = bf16[4,2,80,768]{3,2,1,0:T(8,128)(2,1)S(1)} all-to-all(bf16[4,2,80,768]{3,2,1,0:T(8,128)(2,1)S(1)} %copy.21), channel_id=1, replica_groups=mesh['expert'=4,'tensor'=8] {'expert'}, dimensions={0} | all-to-all | bytes 1966080 | tf_op jit(solution)/shard_map/all_to_all | solution.py:52
  41.2 0.1 fusion.75
  41.3 0.0 copy-start.4
  41.3 0.0 copy-start.5
  41.3 10.9 %fusion.18 = bf16[320,8192]{1,0:T(8,128)(2,1)} fusion(bf16[320,768]{1,0:T(8,128)(2,1)S(1)} %bitcast.70, bf16[1,768,8192]{2,1,0:T(8,128)(2,1)} %param.16), kind=kOutput, calls=%fused_computation.17 | convolution fusion | flops 4029153280 | bytes 18317312 | tf_op jit(solution)/shard_map/dot_general | solution.py:58
  52.2 0.0 reduce-scatter.8.cloned.1.call-update
  52.3 0.0 reduce-scatter.6.cloned.1.call-start
  52.3 10.6 %fusion.15 = bf16[320,8192]{1,0:T(8,128)(2,1)} fusion(bf16[320,768]{1,0:T(8,128)(2,1)S(1)} %bitcast.72, bf16[1,768,8192]{2,1,0:T(8,128)(2,1)} %param.15), kind=kOutput, calls=%fused_computation.16 | convolution fusion | flops 4029153280 | bytes 18317312 | tf_op jit(solution)/shard_map/dot_general | solution.py:58
  62.9 0.0 reduce-scatter.6.cloned.1.call-update
  63.0 0.0 reduce-scatter.4.cloned.1.call-start
  63.0 11.2 %fusion.12 = bf16[320,8192]{1,0:T(8,128)(2,1)} fusion(bf16[320,768]{1,0:T(8,128)(2,1)S(1)} %bitcast.73, bf16[1,768,8192]{2,1,0:T(8,128)(2,1)} %param.14), kind=kOutput, calls=%fused_computation.15 | convolution fusion | flops 4029153280 | bytes 18317312 | tf_op jit(solution)/shard_map/dot_general | solution.py:58
  74.3 0.0 reduce-scatter.4.cloned.1.call-update
  74.3 0.0 all-gather.12.cloned.1.call-start
  74.3 0.5 all-gather.12.cloned.1.call-update
  74.9 0.0 all-gather.14.cloned.1.call-start
  74.9 0.5 all-gather.14.cloned.1.call-update
  75.4 0.0 all-gather.6.cloned.1.call-start
  75.5 32.4 %reduce-scatter.8.cloned.1.call-done = bf16[320,1024]{1,0:T(8,128)(2,1)} async-done(((bf16[320,8192]{1,0:T(8,128)(2,1)}), bf16[320,1024]{1,0:T(8,128)(2,1)}) %reduce-scatter.8.cloned.1.call-update) | async-done | bytes 655376 | tf_op jit(solution)/shard_map/reduce_scatter | solution.py:59
  107.9 60.4 %reduce-scatter.6.cloned.1.call-done = bf16[320,1024]{1,0:T(8,128)(2,1)} async-done(((bf16[320,8192]{1,0:T(8,128)(2,1)}), bf16[320,1024]{1,0:T(8,128)(2,1)}) %reduce-scatter.6.cloned.1.call-update) | async-done | bytes 655376 | tf_op jit(solution)/shard_map/reduce_scatter | solution.py:59
  168.3 60.4 %reduce-scatter.4.cloned.1.call-done = bf16[320,1024]{1,0:T(8,128)(2,1)} async-done(((bf16[320,8192]{1,0:T(8,128)(2,1)}), bf16[320,1024]{1,0:T(8,128)(2,1)}) %reduce-scatter.4.cloned.1.call-update) | async-done | bytes 655376 | tf_op jit(solution)/shard_map/reduce_scatter | solution.py:59
  228.7 0.0 copy-done.7
  228.7 0.0 copy-done.9
  228.7 3.6 multiply_convert_fusion.2
  232.3 0.0 all-gather.6.cloned.1.call-update
  232.4 0.0 all-gather.10.cloned.1.call-start
  232.4 0.7 all-gather.10.cloned.1.call-update
  233.1 0.2 all-gather.8.cloned.1.call-start
  233.3 0.5 all-gather.8.cloned.1.call-update
  233.9 32.0 %all-gather.12.cloned.1.call-done = bf16[320,6144]{1,0:T(8,128)(2,1)} async-done(((bf16[320,768]{1,0:T(8,128)(2,1)}), bf16[320,6144]{1,0:T(8,128)(2,1)}) %all-gather.12.cloned.1.call-update) | async-done | bytes 3932176 | tf_op jit(solution)/shard_map/all_gather | solution.py:63
  265.9 12.1 %convert_bitcast_fusion.2 = bf16[1,6144,1024]{2,1,0:T(8,128)(2,1)} fusion(bf16[320,6144]{1,0:T(8,128)(2,1)} %all-gather.12.cloned.1.call-done, bf16[320,1024]{1,0:T(8,128)(2,1)} %get-tuple-element.10), kind=kOutput, calls=%fused_computation.14 | convolution fusion | flops 4032823296 | bytes 17170432 | tf_op jit(solution)/shard_map/dot_general | solution.py:18
  278.0 0.0 copy-done.11
  278.0 9.7 %convert_bitcast_fusion.1 = bf16[1,6144,1024]{2,1,0:T(8,128)(2,1)} fusion(bf16[320,6144]{1,0:T(8,128)(2,1)S(1)} %copy-done.11, bf16[320,1024]{1,0:T(8,128)(2,1)S(1)} %copy-done.2), kind=kOutput, calls=%fused_computation.13 | convolution fusion | flops 4032823296 | bytes 17170432 | tf_op jit(solution)/shard_map/dot_general | solution.py:18
  287.7 15.4 %all-gather.14.cloned.1.call-done = bf16[320,6144]{1,0:T(8,128)(2,1)} async-done(((bf16[320,768]{1,0:T(8,128)(2,1)}), bf16[320,6144]{1,0:T(8,128)(2,1)}) %all-gather.14.cloned.1.call-update) | async-done | bytes 3932176 | tf_op jit(solution)/shard_map/all_gather | solution.py:63
  303.1 11.8 %convert_bitcast_fusion = bf16[1,6144,1024]{2,1,0:T(8,128)(2,1)} fusion(bf16[320,6144]{1,0:T(8,128)(2,1)} %all-gather.14.cloned.1.call-done, bf16[320,1024]{1,0:T(8,128)(2,1)S(1)} %copy-done.3), kind=kOutput, calls=%fused_computation.12 | convolution fusion | flops 4032823296 | bytes 17170432 | tf_op jit(solution)/shard_map/dot_general | solution.py:18
  314.9 31.0 %all-gather.6.cloned.1.call-done = bf16[320,8192]{1,0:T(8,128)(2,1)} async-done(((bf16[320,1024]{1,0:T(8,128)(2,1)}), bf16[320,8192]{1,0:T(8,128)(2,1)}) %all-gather.6.cloned.1.call-update) | async-done | bytes 5242896 | tf_op jit(solution)/shard_map/all_gather | solution.py:63
  345.9 11.2 %fusion.30 = bf16[320,768]{1,0:T(8,128)(2,1)} fusion(bf16[320,8192]{1,0:T(8,128)(2,1)} %all-gather.6.cloned.1.call-done, bf16[1,768,8192]{2,1,0:T(8,128)(2,1)} %param.16), kind=kOutput, calls=%fused_computation.32 | convolution fusion | flops 4026777600 | bytes 18317312 | tf_op jit(solution)/shard_map/dot_general | solution.py:66
  357.1 4.6 all-to-all-start.1
  361.7 27.1 %all-gather.10.cloned.1.call-done = bf16[320,8192]{1,0:T(8,128)(2,1)} async-done(((bf16[320,1024]{1,0:T(8,128)(2,1)}), bf16[320,8192]{1,0:T(8,128)(2,1)}) %all-gather.10.cloned.1.call-update) | async-done | bytes 5242896 | tf_op jit(solution)/shard_map/all_gather | solution.py:63
  388.8 9.1 %fusion.4 = f32[320,768]{1,0:T(8,128)S(1)} fusion(bf16[320,8192]{1,0:T(8,128)(2,1)} %all-gather.10.cloned.1.call-done, bf16[1,768,8192]{2,1,0:T(8,128)(2,1)} %param.15), kind=kOutput, calls=%fused_computation.4 | convolution fusion | flops 4026531840 | bytes 18808832 | tf_op jit(solution)/shard_map/dot_general | solution.py:66
  397.9 0.0 copy-start.6
  397.9 33.8 %all-gather.8.cloned.1.call-done = bf16[320,8192]{1,0:T(8,128)(2,1)} async-done(((bf16[320,1024]{1,0:T(8,128)(2,1)}), bf16[320,8192]{1,0:T(8,128)(2,1)}) %all-gather.8.cloned.1.call-update) | async-done | bytes 5242896 | tf_op jit(solution)/shard_map/all_gather | solution.py:63
  431.7 11.3 %fusion.27 = bf16[320,768]{1,0:T(8,128)(2,1)} fusion(f32[320,768]{1,0:T(8,128)S(1)} %fusion.4, bf16[320,8192]{1,0:T(8,128)(2,1)} %all-gather.8.cloned.1.call-done, bf16[1,768,8192]{2,1,0:T(8,128)(2,1)} %param.14), kind=kOutput, calls=%fused_computation.31 | convolution fusion | flops 4027023360 | bytes 19300352 | tf_op jit(solution)/shard_map/dot_general | solution.py:66
  443.0 0.0 all-to-all-done.1
  443.0 4.7 %all-to-all-start.2 = ((bf16[4,80,768]{2,1,0:T(8,128)(2,1)}), bf16[4,80,768]{2,1,0:T(8,128)(2,1)S(1)}, u32[]{:S(2)}, u32[]{:S(2)}) async-start(bf16[4,80,768]{2,1,0:T(8,128)(2,1)} %bitcast.14), calls=%async_computation.5 | async-start | bytes 983040 | tf_op jit(solution)/shard_map/all_to_all | solution.py:71
  447.7 1.1 multiply_reduce_fusion
  448.8 0.0 copy-done.6
  448.8 1.1 fusion.21
  449.9 0.1 copy.24
  449.9 13.4 %psum.7 = f32[128,4]{0,1:T(4,128)S(1)} all-reduce(f32[128,4]{0,1:T(4,128)S(1)} %bitcast.78), channel_id=1, replica_groups=mesh['expert'=4,'tensor'=8] {'tensor'}, use_global_device_ids=true, to_apply=%region_6.7 | all-reduce | flops 512 | bytes 4096 | tf_op jit(solution)/shard_map/psum | solution.py:107
  463.4 0.0 copy-done.10
  463.4 0.6 subtract_multiply_fusion
  464.0 0.0 all-to-all-done.2
  464.0 1.0 fusion.35
  (19 shorter events, 0.1 us)
Async XLA Ops:
  7.2 2.7 copy-start
  7.2 100.7 %reduce-scatter.8.cloned.1.call-start = ((), (), s32[]{:S(2)}) async-start(), calls=%async_computation.9 | async-start | bytes 5898240 | tf_op jit(solution)/shard_map/reduce_scatter | solution.py:59
  41.3 11.0 %copy-start.4 = (bf16[4,1,80,768]{3,2,1,0:T(8,128)(2,1)}, bf16[4,1,80,768]{3,2,1,0:T(8,128)(2,1)S(1)}, u32[]{:S(2)}) copy-start(bf16[4,1,80,768]{3,2,1,0:T(8,128)(2,1)S(1)} %get-tuple-element.13) | copy-start | bytes 1474564
  41.3 21.7 %copy-start.5 = (bf16[4,1,80,768]{3,2,1,0:T(8,128)(2,1)}, bf16[4,1,80,768]{3,2,1,0:T(8,128)(2,1)S(1)}, u32[]{:S(2)}) copy-start(bf16[4,1,80,768]{3,2,1,0:T(8,128)(2,1)S(1)} %get-tuple-element.14) | copy-start | bytes 1474564
  52.3 116.0 %reduce-scatter.6.cloned.1.call-start = ((), (), s32[]{:S(2)}) async-start(), calls=%async_computation.7 | async-start | bytes 5898240 | tf_op jit(solution)/shard_map/reduce_scatter | solution.py:59
  63.0 165.7 %reduce-scatter.4.cloned.1.call-start = ((), (), s32[]{:S(2)}) async-start(), calls=%async_computation.6 | async-start | bytes 5898240 | tf_op jit(solution)/shard_map/reduce_scatter | solution.py:59
  74.2 154.5 %copy-start.7 = (f32[1,1024]{1,0:T(1,128)S(1)}, f32[1,1024]{1,0:T(1,128)}, u32[]{:S(2)}) copy-start(f32[1,1024]{1,0:T(1,128)} %param.19) | copy-start | bytes 12292
  74.2 154.5 %copy-start.8 = (f32[1,1024]{1,0:T(1,128)S(1)}, f32[1,1024]{1,0:T(1,128)}, u32[]{:S(2)}) copy-start(f32[1,1024]{1,0:T(1,128)} %param.18) | copy-start | bytes 12292
  74.3 154.5 %copy-start.9 = (f32[1,1024]{1,0:T(1,128)S(1)}, f32[1,1024]{1,0:T(1,128)}, u32[]{:S(2)}) copy-start(f32[1,1024]{1,0:T(1,128)} %param.17) | copy-start | bytes 12292
  74.3 191.6 %all-gather.12.cloned.1.call-start = ((), (), s32[]{:S(2)}) async-start(), calls=%async_computation.12 | async-start | bytes 4423680 | tf_op jit(solution)/shard_map/all_gather | solution.py:63
  74.9 228.2 %all-gather.14.cloned.1.call-start = ((), (), s32[]{:S(2)}) async-start(), calls=%async_computation.13 | async-start | bytes 4423680 | tf_op jit(solution)/shard_map/all_gather | solution.py:63
  75.4 270.4 %all-gather.6.cloned.1.call-start = ((), (), s32[]{:S(2)}) async-start(), calls=%async_computation.8 | async-start | bytes 5898240 | tf_op jit(solution)/shard_map/all_gather | solution.py:63
  232.4 156.4 %all-gather.10.cloned.1.call-start = ((), (), s32[]{:S(2)}) async-start(), calls=%async_computation.11 | async-start | bytes 5898240 | tf_op jit(solution)/shard_map/all_gather | solution.py:63
  233.1 198.6 %all-gather.8.cloned.1.call-start = ((), (), s32[]{:S(2)}) async-start(), calls=%async_computation.10 | async-start | bytes 5898240 | tf_op jit(solution)/shard_map/all_gather | solution.py:63
  233.9 44.1 %copy-start.2 = (bf16[320,1024]{1,0:T(8,128)(2,1)S(1)}, bf16[320,1024]{1,0:T(8,128)(2,1)}, u32[]{:S(2)}) copy-start(bf16[320,1024]{1,0:T(8,128)(2,1)} %get-tuple-element.12) | copy-start | bytes 1966084
  265.9 12.1 %copy-start.11 = (bf16[320,6144]{1,0:T(8,128)(2,1)S(1)}, bf16[320,6144]{1,0:T(8,128)(2,1)}, u32[]{:S(2)}) copy-start(bf16[320,6144]{1,0:T(8,128)(2,1)} %all-gather.12.cloned.1.call-done) | copy-start | bytes 11796484
  278.0 25.1 %copy-start.3 = (bf16[320,1024]{1,0:T(8,128)(2,1)S(1)}, bf16[320,1024]{1,0:T(8,128)(2,1)}, u32[]{:S(2)}) copy-start(bf16[320,1024]{1,0:T(8,128)(2,1)} %get-tuple-element.11) | copy-start | bytes 1966084
  357.1 85.9 %all-to-all-start.1 = ((bf16[4,80,768]{2,1,0:T(8,128)(2,1)}), bf16[4,80,768]{2,1,0:T(8,128)(2,1)S(1)}, u32[]{:S(2)}, u32[]{:S(2)}) async-start(bf16[4,80,768]{2,1,0:T(8,128)(2,1)} %bitcast.12), calls=%async_computation.3 | async-start | bytes 983040 | tf_op jit(solution)/shard_map/all_to_all | solution.py:71
  397.9 50.9 %copy-start.6 = (bf16[128,768]{1,0:T(8,128)(2,1)S(1)}, bf16[128,768]{1,0:T(8,128)(2,1)}, u32[]{:S(2)}) copy-start(bf16[128,768]{1,0:T(8,128)(2,1)} %param.11) | copy-start | bytes 589828
  431.7 33.3 %copy-start.1 = (bf16[128,768]{1,0:T(8,128)(2,1)S(1)}, bf16[128,768]{1,0:T(8,128)(2,1)}, u32[]{:S(2)}) copy-start(bf16[128,768]{1,0:T(8,128)(2,1)} %param.10) | copy-start | bytes 589828
  443.0 20.4 %copy-start.10 = (s32[128,2]{0,1:T(2,128)S(1)}, s32[128,2]{0,1:T(2,128)}, u32[]{:S(2)}) copy-start(s32[128,2]{0,1:T(2,128)} %param.12) | copy-start | bytes 3076
  443.0 21.0 %all-to-all-start.2 = ((bf16[4,80,768]{2,1,0:T(8,128)(2,1)}), bf16[4,80,768]{2,1,0:T(8,128)(2,1)S(1)}, u32[]{:S(2)}, u32[]{:S(2)}) async-start(bf16[4,80,768]{2,1,0:T(8,128)(2,1)} %bitcast.14), calls=%async_computation.5 | async-start | bytes 983040 | tf_op jit(solution)/shard_map/all_to_all | solution.py:71
Sparse Core Ops, SparseCore 0:
  52.4 55.4 reduce-scatter.7
  111.9 56.3 reduce-scatter.5
  172.3 56.3 reduce-scatter.3
  230.5 35.4 all-gather.11
  267.7 35.3 all-gather.13
  304.9 40.9 all-gather.5
  347.8 40.9 all-gather.9
  390.7 40.9 all-gather.7
